TPU v7x, 32 devices: a whole 2x2x4 slice. The times are simulated.
32 devices in a mesh: row: 4 (over z), col: 8 (over y, x, core).
Axes of the slice: x: 2, y: 2, z: 4, core: 2. Of those that a mesh axis runs over, the one named last changes fastest.
Arguments:
- a_vals: bfloat16 [4, 8, 4, 8, 128, 128], P('row', 'col'), may hold values from -0.5 to 0.5
- a_rows: int32 [4, 8, 4, 8], P('row', 'col'), may hold values from 0 to 15
- a_cols: int32 [4, 8, 4, 8], P('row', 'col'), may hold values from 0 to 1
- a_live: int32 [4, 8, 4], P('row', 'col'), may hold values from 1 to 8, as said below
- p_vals: bfloat16 [64, 3, 128, 128], P(('row', 'col')), may hold values from -1 to 1
- p_cols: int32 [64, 3], replicated, may hold values from 0 to 15, as said below
Outputs:
- coarse_op: float32 [16, 16, 128, 128], P('col', 'row')
Inputs may be any that keep to these rules, and one draw needn't show every extreme that they name: Only slots t < a_live[r, c, s] carry blocks of A; the values in the other slots are not part of A. In every draw some grid position has all its sections full. `p_cols`: the 3 coarse block columns of a fine block row i are distinct and lie in the 4 coarse blocks from (i // 16) * 4 on.
All inputs are finite; a program needn't handle non-finite values.
Results may differ from a plain program's by a relative error of at most 0.0029.
Values may be sent and summed in bfloat16 or wider, within the bound.
No kernel may reach another device: no remote copies, remote signals or barrier semaphores. Data moves between devices by JAX's collectives and lax.ppermute only.
A program may use at most 128 MiB of HBM per device.

v0:
```python
import jax
import jax.numpy as jnp
from jax import lax
from jax.sharding import PartitionSpec as P

CROW = 4


def local(a_vals, a_rows, a_cols, a_live, p_vals, p_cols):
    row_count = lax.axis_size("row")
    col_count = lax.axis_size("col")
    grid_row = lax.axis_index("row")
    grid_col = lax.axis_index("col")
    segment = p_vals.shape[0]
    per_row = p_vals.shape[1]
    block_size = p_vals.shape[2]
    slot_count = a_vals.shape[3]
    section_vals = a_vals.reshape(row_count, slot_count, block_size, block_size)
    section_rows = a_rows.reshape(row_count, slot_count)
    section_cols = a_cols.reshape(row_count, slot_count)
    section_live = a_live.reshape(row_count)
    fine_span = segment * col_count
    coarse_total = CROW * row_count
    left_all = lax.all_gather(p_vals, "col", axis=0, tiled=True)
    left_coarse = (
        lax.dynamic_slice_in_dim(p_cols, grid_row * fine_span, fine_span, 0) - grid_row * CROW
    )
    right_coarse = lax.dynamic_index_in_dim(
        p_cols.reshape(row_count, col_count, segment, per_row), grid_col, 1, keepdims=False
    ).reshape(row_count * segment, per_row)
    initial = jnp.zeros((coarse_total, CROW, block_size, block_size), jnp.float32)
    row_labels = lax.iota(jnp.int32, CROW)
    col_labels = lax.iota(jnp.int32, coarse_total)

    def add_slots(partial_value, values, fine_rows, source_index, usable, source, source_coarse):
        right_blocks = jnp.take(source, source_index, axis=0)
        products = jnp.einsum(
            "sij,spjk->spik", values, right_blocks, preferred_element_type=jnp.float32
        )
        products = jnp.where(usable[:, None, None, None], products, 0.0).astype(jnp.bfloat16)
        left_blocks = jnp.take(left_all, fine_rows, axis=0)
        coarse_row = jnp.take(left_coarse, fine_rows, axis=0)
        row_pick = (coarse_row[:, :, None] == row_labels[None, None, :]).astype(jnp.bfloat16)
        folded = jnp.einsum(
            "saq,saji->sqji", row_pick, left_blocks, preferred_element_type=jnp.float32
        ).astype(jnp.bfloat16)
        triple = jnp.einsum(
            "sqji,spjk->spqik", folded, products, preferred_element_type=jnp.float32
        )
        coarse_col = jnp.take(source_coarse, source_index, axis=0)
        col_pick = (coarse_col[:, :, None] == col_labels[None, None, :]).astype(jnp.float32)
        flat_terms = triple.reshape(-1, CROW * block_size * block_size)
        flat_pick = col_pick.reshape(-1, coarse_total)
        added = jnp.einsum("sj,sx->jx", flat_pick, flat_terms, precision=lax.Precision.HIGHEST)
        return partial_value + added.reshape(coarse_total, CROW, block_size, block_size)

    def add_section(partial_value, section_at, source, source_coarse, source_start, piece_len):
        values = lax.dynamic_index_in_dim(section_vals, section_at, 0, keepdims=False)
        fine_rows = lax.dynamic_index_in_dim(section_rows, section_at, 0, keepdims=False)
        fine_cols = lax.dynamic_index_in_dim(section_cols, section_at, 0, keepdims=False)
        live_count = lax.dynamic_index_in_dim(section_live, section_at, 0, keepdims=False)
        target = section_at * segment + fine_cols
        inside = (target >= source_start) & (target < source_start + piece_len)
        source_index = jnp.clip(target - source_start, 0, piece_len - 1)
        position = lax.iota(jnp.int32, slot_count)
        usable = inside & (position < live_count)
        return add_slots(
            partial_value, values, fine_rows, source_index, usable, source, source_coarse
        )

    right_all = lax.all_gather(p_vals, "row", axis=0, tiled=True)

    def whole_section(section_at, running):
        return add_section(running, section_at, right_all, right_coarse, 0, row_count * segment)

    partial_value = lax.fori_loop(0, row_count, whole_section, initial)
    return lax.psum_scatter(partial_value, "col", scatter_dimension=0, tiled=True)


def solution(mesh):
    return jax.shard_map(
        local,
        mesh=mesh,
        in_specs=(
            P("row", "col", None, None, None, None),
            P("row", "col", None, None),
            P("row", "col", None, None),
            P("row", "col", None),
            P(("row", "col"), None, None, None),
            P(),
        ),
        out_specs=P("col", "row", None, None),
        check_vma=False,
    )
```

profile of v0, /device:TPU:0, one launch (start us, length us, event | category | flops | bytes accessed | tf_op | source)
XLA Modules:
  0.0 262.2 jit_solution(9492211815750386809)
XLA Ops:
  6.5 0.7 all-gather.2.cloned.1.call-update
  7.3 0.8 reshape.178
  8.1 0.8 constant_dynamic-slice_fusion.2
  9.1 21.5 %all_gather.6 = bf16[8,3,128,128]{3,2,1,0:T(8,128)(2,1)S(1)} all-gather(bf16[2,3,128,128]{3,2,1,0:T(8,128)(2,1)} %param.12), channel_id=1, replica_groups=mesh['row'=4,'col'=8] {'row'}, dimensions={0}, use_global_device_ids=true | all-gather | bytes 983040 | tf_op jit(solution)/shard_map/all_gather | solution.py:71
  30.6 7.1 %all-gather.2.cloned.1.call-done = bf16[16,3,128,128]{3,2,1,0:T(8,128)(2,1)} async-done(((bf16[2,3,128,128]{3,2,1,0:T(8,128)(2,1)}), bf16[16,3,128,128]{3,2,1,0:T(8,128)(2,1)}) %all-gather.2.cloned.1.call-update) | async-done | bytes 1572880 | tf_op jit(solution)/shard_map/all_gather | solution.py:24
  37.7 160.7 %while.14 = (s32[]{:T(128)}, f32[16,4,128,128]{3,0,2,1:T(8,128)}, s32[4,8]{1,0:T(4,128)}, s32[8,3]{1,0:T(8,128)S(1)}, s32[4]{0:T(128)}, /*index=5*/bf16[8,3,128,...) while((s32[]{:T(128)}, f32[16,4,128,128]{3,0,2,1:T(8,128)}, ...), condition=%wide.region_1.2_spmd.clone, body=%wide.region_0.1_spmd.clone.sunk | while | flops 812649216 | bytes 100935528 | solution.py:76
  37.7 1.2 dynamic_slice.65
  38.9 0.7 fusion.56
  39.6 1.3 bitcast_and_fusion.2
  40.9 0.6 gather_fusion.1
  41.5 0.6 gather_fusion.3
  42.3 0.7 gather_fusion.2
  43.0 2.1 gather_fusion
  45.2 0.8 fusion.57
  46.0 5.0 %convolution_bitcast_fusion.2 = f32[8,3,4,128,128]{3,4,2,1,0:T(8,128)} fusion(bf16[8,4,128,128,1]{3,1,2,0,4:T(4,128)(2,1)S(1)} %fusion.57, bf16[8,3,128,128]{3,2,1,0:T(8,128)(2,1)S(1)} %gather_fusion.2, pred[8]{0:T(512)(128)(4,1)S(1)} %compare_and_fusion.3, pred[8]{0:T(512)(128)(4,1)S(1)} %get-tuple-element.331, ...), kind=kOutput, calls=%fused_computation.9.clone.1 | convolution fusion | flops 504496128 | bytes 8388628 | tf_op jit(solution)/shard_map/while/body/eval_jaxpr/sqji,spjk->spqik/dot_general | solution.py:47
  51.0 6.6 %copy.49 = f32[8,3,4,128,128]{4,3,2,1,0:T(8,128)} copy(f32[8,3,4,128,128]{3,4,2,1,0:T(8,128)} %convolution_bitcast_fusion.2) | data formatting | bytes 12582912 | tf_op jit(solution)/shard_map/while/body/eval_jaxpr/sqji,spjk->spqik/transpose | solution.py:47
  57.6 6.8 %reshape.248 = f32[24,65536]{1,0:T(8,128)} reshape(f32[8,3,4,128,128]{4,3,2,1,0:T(8,128)} %copy.49) | data formatting | bytes 12582912 | tf_op jit(solution)/shard_map/while/body/eval_jaxpr/reshape | solution.py:52
  64.4 4.0 %copy.50 = f32[3,8,512,128]{3,2,1,0:T(8,128)S(1)} copy(f32[3,8,512,128]{3,1,2,0:T(8,128)} %bitcast.89) | data formatting | bytes 12582912 | tf_op jit(solution)/shard_map/while
  68.4 7.4 %select_add_fusion.2 = f32[16,4,128,128]{3,0,2,1:T(8,128)S(1)} fusion(f32[16,4,128,128]{3,0,2,1:T(8,128)S(1)} %copy-done, f32[4,128,128,24]{2,1,0,3:T(8,128)S(1)} %bitcast.90, pred[]{:T(512)S(6)} %compare.3, s32[24]{0:T(128)S(1)} %select_n.169), kind=kOutput, calls=%fused_computation.8.clone.1 | convolution fusion | flops 304087424 | bytes 14680161 | tf_op jit(solution)/shard_map/while/body/eval_jaxpr/sj,sx->jx/dot_general | solution.py:54
  75.9 1.9 copy-done.1
  77.8 1.2 dynamic_slice.65
  79.1 0.7 fusion.56
  79.8 1.3 bitcast_and_fusion.2
  81.1 0.6 gather_fusion.1
  81.7 0.6 gather_fusion.3
  82.4 0.7 gather_fusion.2
  83.1 2.1 gather_fusion
  85.4 0.8 fusion.57
  86.2 5.0 %convolution_bitcast_fusion.2 = f32[8,3,4,128,128]{3,4,2,1,0:T(8,128)} fusion(bf16[8,4,128,128,1]{3,1,2,0,4:T(4,128)(2,1)S(1)} %fusion.57, bf16[8,3,128,128]{3,2,1,0:T(8,128)(2,1)S(1)} %gather_fusion.2, pred[8]{0:T(512)(128)(4,1)S(1)} %compare_and_fusion.3, pred[8]{0:T(512)(128)(4,1)S(1)} %get-tuple-element.331, ...), kind=kOutput, calls=%fused_computation.9.clone.1 | convolution fusion | flops 504496128 | bytes 8388628 | tf_op jit(solution)/shard_map/while/body/eval_jaxpr/sqji,spjk->spqik/dot_general | solution.py:47
  91.2 6.6 %copy.49 = f32[8,3,4,128,128]{4,3,2,1,0:T(8,128)} copy(f32[8,3,4,128,128]{3,4,2,1,0:T(8,128)} %convolution_bitcast_fusion.2) | data formatting | bytes 12582912 | tf_op jit(solution)/shard_map/while/body/eval_jaxpr/sqji,spjk->spqik/transpose | solution.py:47
  97.7 6.8 %reshape.248 = f32[24,65536]{1,0:T(8,128)} reshape(f32[8,3,4,128,128]{4,3,2,1,0:T(8,128)} %copy.49) | data formatting | bytes 12582912 | tf_op jit(solution)/shard_map/while/body/eval_jaxpr/reshape | solution.py:52
  104.6 4.0 %copy.50 = f32[3,8,512,128]{3,2,1,0:T(8,128)S(1)} copy(f32[3,8,512,128]{3,1,2,0:T(8,128)} %bitcast.89) | data formatting | bytes 12582912 | tf_op jit(solution)/shard_map/while
  108.6 7.4 %select_add_fusion.2 = f32[16,4,128,128]{3,0,2,1:T(8,128)S(1)} fusion(f32[16,4,128,128]{3,0,2,1:T(8,128)S(1)} %copy-done, f32[4,128,128,24]{2,1,0,3:T(8,128)S(1)} %bitcast.90, pred[]{:T(512)S(6)} %compare.3, s32[24]{0:T(128)S(1)} %select_n.169), kind=kOutput, calls=%fused_computation.8.clone.1 | convolution fusion | flops 304087424 | bytes 14680161 | tf_op jit(solution)/shard_map/while/body/eval_jaxpr/sj,sx->jx/dot_general | solution.py:54
  116.1 1.9 copy-done.1
  118.0 1.2 dynamic_slice.65
  119.2 0.7 fusion.56
  119.9 1.3 bitcast_and_fusion.2
  121.3 0.6 gather_fusion.1
  121.9 0.6 gather_fusion.3
  122.6 0.7 gather_fusion.2
  123.3 2.1 gather_fusion
  125.6 0.8 fusion.57
  126.4 5.0 %convolution_bitcast_fusion.2 = f32[8,3,4,128,128]{3,4,2,1,0:T(8,128)} fusion(bf16[8,4,128,128,1]{3,1,2,0,4:T(4,128)(2,1)S(1)} %fusion.57, bf16[8,3,128,128]{3,2,1,0:T(8,128)(2,1)S(1)} %gather_fusion.2, pred[8]{0:T(512)(128)(4,1)S(1)} %compare_and_fusion.3, pred[8]{0:T(512)(128)(4,1)S(1)} %get-tuple-element.331, ...), kind=kOutput, calls=%fused_computation.9.clone.1 | convolution fusion | flops 504496128 | bytes 8388628 | tf_op jit(solution)/shard_map/while/body/eval_jaxpr/sqji,spjk->spqik/dot_general | solution.py:47
  131.3 6.6 %copy.49 = f32[8,3,4,128,128]{4,3,2,1,0:T(8,128)} copy(f32[8,3,4,128,128]{3,4,2,1,0:T(8,128)} %convolution_bitcast_fusion.2) | data formatting | bytes 12582912 | tf_op jit(solution)/shard_map/while/body/eval_jaxpr/sqji,spjk->spqik/transpose | solution.py:47
  137.9 6.8 %reshape.248 = f32[24,65536]{1,0:T(8,128)} reshape(f32[8,3,4,128,128]{4,3,2,1,0:T(8,128)} %copy.49) | data formatting | bytes 12582912 | tf_op jit(solution)/shard_map/while/body/eval_jaxpr/reshape | solution.py:52
  144.8 4.0 %copy.50 = f32[3,8,512,128]{3,2,1,0:T(8,128)S(1)} copy(f32[3,8,512,128]{3,1,2,0:T(8,128)} %bitcast.89) | data formatting | bytes 12582912 | tf_op jit(solution)/shard_map/while
  148.8 7.4 %select_add_fusion.2 = f32[16,4,128,128]{3,0,2,1:T(8,128)S(1)} fusion(f32[16,4,128,128]{3,0,2,1:T(8,128)S(1)} %copy-done, f32[4,128,128,24]{2,1,0,3:T(8,128)S(1)} %bitcast.90, pred[]{:T(512)S(6)} %compare.3, s32[24]{0:T(128)S(1)} %select_n.169), kind=kOutput, calls=%fused_computation.8.clone.1 | convolution fusion | flops 304087424 | bytes 14680161 | tf_op jit(solution)/shard_map/while/body/eval_jaxpr/sj,sx->jx/dot_general | solution.py:54
  156.3 1.9 copy-done.1
  158.2 1.2 dynamic_slice.65
  159.4 0.7 fusion.56
  160.1 1.3 bitcast_and_fusion.2
  161.4 0.6 gather_fusion.1
  162.1 0.6 gather_fusion.3
  162.8 0.7 gather_fusion.2
  163.5 2.1 gather_fusion
  165.7 0.8 fusion.57
  166.5 5.0 %convolution_bitcast_fusion.2 = f32[8,3,4,128,128]{3,4,2,1,0:T(8,128)} fusion(bf16[8,4,128,128,1]{3,1,2,0,4:T(4,128)(2,1)S(1)} %fusion.57, bf16[8,3,128,128]{3,2,1,0:T(8,128)(2,1)S(1)} %gather_fusion.2, pred[8]{0:T(512)(128)(4,1)S(1)} %compare_and_fusion.3, pred[8]{0:T(512)(128)(4,1)S(1)} %get-tuple-element.331, ...), kind=kOutput, calls=%fused_computation.9.clone.1 | convolution fusion | flops 504496128 | bytes 8388628 | tf_op jit(solution)/shard_map/while/body/eval_jaxpr/sqji,spjk->spqik/dot_general | solution.py:47
  171.5 6.6 %copy.49 = f32[8,3,4,128,128]{4,3,2,1,0:T(8,128)} copy(f32[8,3,4,128,128]{3,4,2,1,0:T(8,128)} %convolution_bitcast_fusion.2) | data formatting | bytes 12582912 | tf_op jit(solution)/shard_map/while/body/eval_jaxpr/sqji,spjk->spqik/transpose | solution.py:47
  178.1 6.8 %reshape.248 = f32[24,65536]{1,0:T(8,128)} reshape(f32[8,3,4,128,128]{4,3,2,1,0:T(8,128)} %copy.49) | data formatting | bytes 12582912 | tf_op jit(solution)/shard_map/while/body/eval_jaxpr/reshape | solution.py:52
  184.9 4.0 %copy.50 = f32[3,8,512,128]{3,2,1,0:T(8,128)S(1)} copy(f32[3,8,512,128]{3,1,2,0:T(8,128)} %bitcast.89) | data formatting | bytes 12582912 | tf_op jit(solution)/shard_map/while
  189.0 7.4 %select_add_fusion.2 = f32[16,4,128,128]{3,0,2,1:T(8,128)S(1)} fusion(f32[16,4,128,128]{3,0,2,1:T(8,128)S(1)} %copy-done, f32[4,128,128,24]{2,1,0,3:T(8,128)S(1)} %bitcast.90, pred[]{:T(512)S(6)} %compare.3, s32[24]{0:T(128)S(1)} %select_n.169), kind=kOutput, calls=%fused_computation.8.clone.1 | convolution fusion | flops 304087424 | bytes 14680161 | tf_op jit(solution)/shard_map/while/body/eval_jaxpr/sj,sx->jx/dot_general | solution.py:54
  196.4 1.9 copy-done.1
  198.3 5.5 %copy.22 = f32[16,4,128,128]{3,2,1,0:T(8,128)} copy(f32[16,4,128,128]{3,0,2,1:T(8,128)} %get-tuple-element.204) | data formatting | bytes 8388608 | tf_op jit(solution)/shard_map/while | solution.py:76
  203.9 51.5 %reduce-scatter.2.cloned.1.call-done = f32[2,4,128,128]{3,2,1,0:T(8,128)} async-done(((f32[16,4,128,128]{3,2,1,0:T(8,128)}), f32[2,4,128,128]{3,2,1,0:T(8,128)}) %reduce-scatter.2.cloned.1.call-update) | async-done | bytes 524304 | tf_op jit(solution)/shard_map/reduce_scatter | solution.py:77
  (52 shorter events, 1.9 us)
Async XLA Ops:
  6.5 31.1 %all-gather.2.cloned.1.call-start = ((), (), s32[]{:S(2)}) async-start(), calls=%async_computation.1 | async-start | bytes 1769472 | tf_op jit(solution)/shard_map/all_gather | solution.py:24
  7.3 248.1 %reduce-scatter.2.cloned.1.call-start = ((), (), s32[]{:S(2)}) async-start(), calls=%async_computation.2 | async-start | bytes 4718592 | tf_op jit(solution)/shard_map/reduce_scatter | solution.py:77
  64.4 4.0 %copy-start = (f32[16,4,128,128]{3,0,2,1:T(8,128)S(1)}, f32[16,4,128,128]{3,0,2,1:T(8,128)}, u32[]{:S(2)}) copy-start(f32[16,4,128,128]{3,0,2,1:T(8,128)} %get-tuple-element.346) | copy-start | bytes 12582916 | tf_op jit(solution)/shard_map/while
  75.9 1.9 copy-start.1
  104.6 4.0 %copy-start = (f32[16,4,128,128]{3,0,2,1:T(8,128)S(1)}, f32[16,4,128,128]{3,0,2,1:T(8,128)}, u32[]{:S(2)}) copy-start(f32[16,4,128,128]{3,0,2,1:T(8,128)} %get-tuple-element.346) | copy-start | bytes 12582916 | tf_op jit(solution)/shard_map/while
  116.1 1.9 copy-start.1
  144.8 4.0 %copy-start = (f32[16,4,128,128]{3,0,2,1:T(8,128)S(1)}, f32[16,4,128,128]{3,0,2,1:T(8,128)}, u32[]{:S(2)}) copy-start(f32[16,4,128,128]{3,0,2,1:T(8,128)} %get-tuple-element.346) | copy-start | bytes 12582916 | tf_op jit(solution)/shard_map/while
  156.2 1.9 copy-start.1
  184.9 4.0 %copy-start = (f32[16,4,128,128]{3,0,2,1:T(8,128)S(1)}, f32[16,4,128,128]{3,0,2,1:T(8,128)}, u32[]{:S(2)}) copy-start(f32[16,4,128,128]{3,0,2,1:T(8,128)} %get-tuple-element.346) | copy-start | bytes 12582916 | tf_op jit(solution)/shard_map/while
  196.4 1.9 copy-start.1
Sparse Core Ops, SparseCore 0:
  9.2 28.3 all-gather.1
  204.0 51.3 reduce-scatter.1
where the time goes:
time: 263 us; the launch traced here: 262 us
  local copies, waits for them, and re-layouts  106 us (40%)
  waiting for transfers between devices  59.3 us (23%)
  matrix products  52.8 us (20%)
  blocking collectives  21.5 us (8%)
  between operations  13.4 us (5%)
  other arithmetic  9.08 us (3%)
    reduce_scatter x1, waiting for transfers between devices, local(): lax.psum_scatter(partial_value, 'col', scatter_dimension=0, tiled=True)  51.5 us
    dot_general x4, matrix products, add_slots(): jnp.einsum('sj,sx->jx', flat_pick, flat_terms, precision=lax.Precision.HI...  29.8 us
    reshape x4, local copies, waits for them, and re-layouts, add_slots(): flat_terms = triple.reshape(-1, CROW * block_size * block_size)  27.4 us
    transpose x4, local copies, waits for them, and re-layouts, add_slots(): jnp.einsum('sqji,spjk->spqik', folded, products, preferred_element_type=j...  26.3 us
    while x20, local copies, waits for them, and re-layouts  23.8 us
    all_gather x1, blocking collectives, local(): right_all = lax.all_gather(p_vals, 'row', axis=0, tiled=True)  21.5 us
    dot_general x4, matrix products, add_slots(): jnp.einsum('sqji,spjk->spqik', folded, products, preferred_element_type=j...  19.9 us
    gather x4, local copies, waits for them, and re-layouts, add_slots(): left_blocks = jnp.take(left_all, fine_rows, axis=0)  8.43 us
  transfers between devices with their start and end apart: 2, of which 2 were waited for; matrix products, arithmetic and copies ran while one was open for 1% of the time, Pallas kernels for 0%

commit v1 on v0

--- a/solution.py
+++ b/solution.py
@@ -68,7 +68,17 @@
             partial_value, values, fine_rows, source_index, usable, source, source_coarse
         )
 
-    right_all = lax.all_gather(p_vals, "row", axis=0, tiled=True)
+    devices, here, extent = (lax.axis_size("row"), lax.axis_index("row"), p_vals.shape[0])
+    right = [(i, (i + 1) % devices) for i in range(devices)]
+    right_all = jnp.zeros(
+        (*p_vals.shape[:0], devices * extent, *p_vals.shape[0 + 1 :]), p_vals.dtype
+    )
+    held = p_vals
+    for step in range(devices):
+        owner = (here - step) % devices
+        right_all = lax.dynamic_update_slice_in_dim(right_all, held, owner * extent, axis=0)
+        if step < devices - 1:
+            held = lax.ppermute(held, "row", right)
 
     def whole_section(section_at, running):
         return add_section(running, section_at, right_all, right_coarse, 0, row_count * segment)

time: 263 us -> 264 us (level)
  blocking collectives: 21.5 us -> 0 us
  waiting for transfers between devices: 59.3 us -> 76.5 us
  starting transfers between devices: 0.04 us -> 3.12 us
    all_gather x1 -> x0, blocking collectives: 21.5 us -> none  [local(): right_all = lax.all_gather(p_vals, 'row', axis=0, tiled=True)]
    ppermute x0 -> x3, waiting for transfers between devices: none -> 19.5 us  [local(): held = lax.ppermute(held, 'row', right)]
    ppermute x0 -> x3, starting transfers between devices: none -> 3.08 us  [local(): held = lax.ppermute(held, 'row', right)]
  transfers between devices with their start and end apart: 2 -> 5, of which waited for: 2 -> 5; matrix products, arithmetic and copies ran while one was open for 1% -> 1% of each run, Pallas kernels for 0% -> 0%
where the time goes in v1:
time: 264 us; the launch traced here: 263 us
  local copies, waits for them, and re-layouts  107 us (41%)
  waiting for transfers between devices  76.5 us (29%)
  matrix products  52.9 us (20%)
  between operations  13.4 us (5%)
  other arithmetic  9.38 us (4%)
  starting transfers between devices  3.12 us (1%)
    reduce_scatter x1, waiting for transfers between devices, local(): lax.psum_scatter(partial_value, 'col', scatter_dimension=0, tiled=True)  51.4 us
    dot_general x4, matrix products, add_slots(): jnp.einsum('sj,sx->jx', flat_pick, flat_terms, precision=lax.Precision.HI...  29.8 us
    reshape x4, local copies, waits for them, and re-layouts, add_slots(): flat_terms = triple.reshape(-1, CROW * block_size * block_size)  27.4 us
    transpose x4, local copies, waits for them, and re-layouts, add_slots(): jnp.einsum('sqji,spjk->spqik', folded, products, preferred_element_type=j...  26.3 us
    while x20, local copies, waits for them, and re-layouts  23.8 us
    dot_general x4, matrix products, add_slots(): jnp.einsum('sqji,spjk->spqik', folded, products, preferred_element_type=j...  20 us
    ppermute x3, waiting for transfers between devices, local(): held = lax.ppermute(held, 'row', right)  19.5 us
    gather x4, local copies, waits for them, and re-layouts, add_slots(): left_blocks = jnp.take(left_all, fine_rows, axis=0)  8.43 us
  transfers between devices with their start and end apart: 5, of which 5 were waited for; matrix products, arithmetic and copies ran while one was open for 1% of the time, Pallas kernels for 0%

profile of v1, /device:TPU:0, one launch (start us, length us, event | category | flops | bytes accessed | tf_op | source)
XLA Modules:
  0.0 262.7 jit_solution(5231867114966661604)
XLA Ops:
  6.5 0.7 all-gather.2.cloned.1.call-update
  7.3 3.1 %collective-permute-start = (bf16[2,3,128,128]{3,2,1,0:T(8,128)(2,1)}, bf16[2,3,128,128]{3,2,1,0:T(8,128)(2,1)S(1)}, u32[]{:S(2)}, u32[]{:S(2)}) collective-permute-start(bf16[2,3,128,128]{3,2,1,0:T(8,128)(2,1)} %param.12), channel_id=1, source_target_pairs={{0,8},{8,16},{16,24},{24,0},{1,9},{9,17},{17,25},{25,1},{2,10},{10... | collective-permute-start | bytes 589832 | tf_op jit(solution)/shard_map/ppermute | solution.py:81
  10.4 0.8 reshape.178
  11.2 0.8 constant_dynamic-slice_fusion.2
  12.3 1.0 constant_dynamic-update-slice_fusion.3
  13.3 4.2 %collective-permute-done = bf16[2,3,128,128]{3,2,1,0:T(8,128)(2,1)S(1)} collective-permute-done((bf16[2,3,128,128]{3,2,1,0:T(8,128)(2,1)}, bf16[2,3,128,128]{3,2,1,0:T(8,128)(2,1)S(1)}, u32[]{:S(2)}, u32[]{:S(2)}) %collective-permute-start) | collective-permute-done | bytes 196640 | tf_op jit(solution)/shard_map/ppermute | solution.py:81
  17.5 7.9 %collective-permute-done.1 = bf16[2,3,128,128]{3,2,1,0:T(8,128)(2,1)S(1)} collective-permute-done((bf16[2,3,128,128]{3,2,1,0:T(8,128)(2,1)S(1)}, bf16[2,3,128,128]{3,2,1,0:T(8,128)(2,1)S(1)}, u32[]{:S(2)}, u32[]{:S(2)}) %collective-permute-start.1) | collective-permute-done | bytes 196640 | tf_op jit(solution)/shard_map/ppermute | solution.py:81
  25.5 7.4 %collective-permute-done.2 = bf16[2,3,128,128]{3,2,1,0:T(8,128)(2,1)S(1)} collective-permute-done((bf16[2,3,128,128]{3,2,1,0:T(8,128)(2,1)S(1)}, bf16[2,3,128,128]{3,2,1,0:T(8,128)(2,1)S(1)}, u32[]{:S(2)}, u32[]{:S(2)}) %collective-permute-start.2) | collective-permute-done | bytes 196640 | tf_op jit(solution)/shard_map/ppermute | solution.py:81
  32.9 4.8 %all-gather.2.cloned.1.call-done = bf16[16,3,128,128]{3,2,1,0:T(8,128)(2,1)} async-done(((bf16[2,3,128,128]{3,2,1,0:T(8,128)(2,1)}), bf16[16,3,128,128]{3,2,1,0:T(8,128)(2,1)}) %all-gather.2.cloned.1.call-update) | async-done | bytes 1572880 | tf_op jit(solution)/shard_map/all_gather | solution.py:24
  37.7 161.2 %while.14 = (s32[]{:T(128)}, f32[16,4,128,128]{3,0,2,1:T(8,128)}, s32[4,8]{1,0:T(4,128)}, s32[8,3]{1,0:T(8,128)S(1)}, s32[4]{0:T(128)}, /*index=5*/bf16[8,3,128,...) while((s32[]{:T(128)}, f32[16,4,128,128]{3,0,2,1:T(8,128)}, ...), condition=%wide.region_1.2_spmd.clone, body=%wide.region_0.1_spmd.clone.sunk | while | flops 812649216 | bytes 100935528 | solution.py:86
  37.7 1.3 dynamic_slice.65
  38.9 0.7 fusion.56
  39.6 1.3 bitcast_and_fusion.2
  41.0 0.6 gather_fusion.1
  42.4 0.7 gather_fusion.2
  43.1 2.1 gather_fusion
  45.3 0.8 fusion.57
  46.1 5.0 %convolution_bitcast_fusion.2 = f32[8,3,4,128,128]{3,4,2,1,0:T(8,128)} fusion(bf16[8,4,128,128,1]{3,1,2,0,4:T(4,128)(2,1)S(1)} %fusion.57, bf16[8,3,128,128]{3,2,1,0:T(8,128)(2,1)S(1)} %gather_fusion.2, pred[8]{0:T(512)(128)(4,1)S(1)} %compare_and_fusion.3, pred[8]{0:T(512)(128)(4,1)S(1)} %get-tuple-element.331, ...), kind=kOutput, calls=%fused_computation.9.clone.1 | convolution fusion | flops 504496128 | bytes 8388628 | tf_op jit(solution)/shard_map/while/body/eval_jaxpr/sqji,spjk->spqik/dot_general | solution.py:47
  51.1 6.6 %copy.49 = f32[8,3,4,128,128]{4,3,2,1,0:T(8,128)} copy(f32[8,3,4,128,128]{3,4,2,1,0:T(8,128)} %convolution_bitcast_fusion.2) | data formatting | bytes 12582912 | tf_op jit(solution)/shard_map/while/body/eval_jaxpr/sqji,spjk->spqik/transpose | solution.py:47
  57.7 6.9 %reshape.248 = f32[24,65536]{1,0:T(8,128)} reshape(f32[8,3,4,128,128]{4,3,2,1,0:T(8,128)} %copy.49) | data formatting | bytes 12582912 | tf_op jit(solution)/shard_map/while/body/eval_jaxpr/reshape | solution.py:52
  64.6 4.0 %copy.50 = f32[3,8,512,128]{3,2,1,0:T(8,128)S(1)} copy(f32[3,8,512,128]{3,1,2,0:T(8,128)} %bitcast.89) | data formatting | bytes 12582912 | tf_op jit(solution)/shard_map/while
  68.6 7.4 %select_add_fusion.2 = f32[16,4,128,128]{3,0,2,1:T(8,128)S(1)} fusion(f32[16,4,128,128]{3,0,2,1:T(8,128)S(1)} %copy-done, f32[4,128,128,24]{2,1,0,3:T(8,128)S(1)} %bitcast.90, pred[]{:T(512)S(6)} %compare.7, s32[24]{0:T(128)S(1)} %select_n.208), kind=kOutput, calls=%fused_computation.8.clone.1 | convolution fusion | flops 304087424 | bytes 14680161 | tf_op jit(solution)/shard_map/while/body/eval_jaxpr/sj,sx->jx/dot_general | solution.py:54
  76.0 1.9 copy-done.1
  78.0 1.3 dynamic_slice.65
  79.2 0.7 fusion.56
  79.9 1.3 bitcast_and_fusion.2
  81.3 0.6 gather_fusion.1
  82.7 0.7 gather_fusion.2
  83.4 2.1 gather_fusion
  85.6 0.8 fusion.57
  86.4 5.0 %convolution_bitcast_fusion.2 = f32[8,3,4,128,128]{3,4,2,1,0:T(8,128)} fusion(bf16[8,4,128,128,1]{3,1,2,0,4:T(4,128)(2,1)S(1)} %fusion.57, bf16[8,3,128,128]{3,2,1,0:T(8,128)(2,1)S(1)} %gather_fusion.2, pred[8]{0:T(512)(128)(4,1)S(1)} %compare_and_fusion.3, pred[8]{0:T(512)(128)(4,1)S(1)} %get-tuple-element.331, ...), kind=kOutput, calls=%fused_computation.9.clone.1 | convolution fusion | flops 504496128 | bytes 8388628 | tf_op jit(solution)/shard_map/while/body/eval_jaxpr/sqji,spjk->spqik/dot_general | solution.py:47
  91.4 6.6 %copy.49 = f32[8,3,4,128,128]{4,3,2,1,0:T(8,128)} copy(f32[8,3,4,128,128]{3,4,2,1,0:T(8,128)} %convolution_bitcast_fusion.2) | data formatting | bytes 12582912 | tf_op jit(solution)/shard_map/while/body/eval_jaxpr/sqji,spjk->spqik/transpose | solution.py:47
  98.0 6.9 %reshape.248 = f32[24,65536]{1,0:T(8,128)} reshape(f32[8,3,4,128,128]{4,3,2,1,0:T(8,128)} %copy.49) | data formatting | bytes 12582912 | tf_op jit(solution)/shard_map/while/body/eval_jaxpr/reshape | solution.py:52
  104.9 4.0 %copy.50 = f32[3,8,512,128]{3,2,1,0:T(8,128)S(1)} copy(f32[3,8,512,128]{3,1,2,0:T(8,128)} %bitcast.89) | data formatting | bytes 12582912 | tf_op jit(solution)/shard_map/while
  108.9 7.4 %select_add_fusion.2 = f32[16,4,128,128]{3,0,2,1:T(8,128)S(1)} fusion(f32[16,4,128,128]{3,0,2,1:T(8,128)S(1)} %copy-done, f32[4,128,128,24]{2,1,0,3:T(8,128)S(1)} %bitcast.90, pred[]{:T(512)S(6)} %compare.7, s32[24]{0:T(128)S(1)} %select_n.208), kind=kOutput, calls=%fused_computation.8.clone.1 | convolution fusion | flops 304087424 | bytes 14680161 | tf_op jit(solution)/shard_map/while/body/eval_jaxpr/sj,sx->jx/dot_general | solution.py:54
  116.3 1.9 copy-done.1
  118.3 1.3 dynamic_slice.65
  119.5 0.7 fusion.56
  120.2 1.3 bitcast_and_fusion.2
  121.6 0.6 gather_fusion.1
  123.0 0.7 gather_fusion.2
  123.7 2.1 gather_fusion
  125.9 0.8 fusion.57
  126.7 5.0 %convolution_bitcast_fusion.2 = f32[8,3,4,128,128]{3,4,2,1,0:T(8,128)} fusion(bf16[8,4,128,128,1]{3,1,2,0,4:T(4,128)(2,1)S(1)} %fusion.57, bf16[8,3,128,128]{3,2,1,0:T(8,128)(2,1)S(1)} %gather_fusion.2, pred[8]{0:T(512)(128)(4,1)S(1)} %compare_and_fusion.3, pred[8]{0:T(512)(128)(4,1)S(1)} %get-tuple-element.331, ...), kind=kOutput, calls=%fused_computation.9.clone.1 | convolution fusion | flops 504496128 | bytes 8388628 | tf_op jit(solution)/shard_map/while/body/eval_jaxpr/sqji,spjk->spqik/dot_general | solution.py:47
  131.7 6.6 %copy.49 = f32[8,3,4,128,128]{4,3,2,1,0:T(8,128)} copy(f32[8,3,4,128,128]{3,4,2,1,0:T(8,128)} %convolution_bitcast_fusion.2) | data formatting | bytes 12582912 | tf_op jit(solution)/shard_map/while/body/eval_jaxpr/sqji,spjk->spqik/transpose | solution.py:47
  138.3 6.9 %reshape.248 = f32[24,65536]{1,0:T(8,128)} reshape(f32[8,3,4,128,128]{4,3,2,1,0:T(8,128)} %copy.49) | data formatting | bytes 12582912 | tf_op jit(solution)/shard_map/while/body/eval_jaxpr/reshape | solution.py:52
  145.2 4.0 %copy.50 = f32[3,8,512,128]{3,2,1,0:T(8,128)S(1)} copy(f32[3,8,512,128]{3,1,2,0:T(8,128)} %bitcast.89) | data formatting | bytes 12582912 | tf_op jit(solution)/shard_map/while
  149.2 7.4 %select_add_fusion.2 = f32[16,4,128,128]{3,0,2,1:T(8,128)S(1)} fusion(f32[16,4,128,128]{3,0,2,1:T(8,128)S(1)} %copy-done, f32[4,128,128,24]{2,1,0,3:T(8,128)S(1)} %bitcast.90, pred[]{:T(512)S(6)} %compare.7, s32[24]{0:T(128)S(1)} %select_n.208), kind=kOutput, calls=%fused_computation.8.clone.1 | convolution fusion | flops 304087424 | bytes 14680161 | tf_op jit(solution)/shard_map/while/body/eval_jaxpr/sj,sx->jx/dot_general | solution.py:54
  156.7 1.9 copy-done.1
  158.6 1.3 dynamic_slice.65
  159.8 0.7 fusion.56
  160.5 1.3 bitcast_and_fusion.2
  161.9 0.6 gather_fusion.1
  163.3 0.7 gather_fusion.2
  164.0 2.1 gather_fusion
  166.2 0.8 fusion.57
  167.0 5.0 %convolution_bitcast_fusion.2 = f32[8,3,4,128,128]{3,4,2,1,0:T(8,128)} fusion(bf16[8,4,128,128,1]{3,1,2,0,4:T(4,128)(2,1)S(1)} %fusion.57, bf16[8,3,128,128]{3,2,1,0:T(8,128)(2,1)S(1)} %gather_fusion.2, pred[8]{0:T(512)(128)(4,1)S(1)} %compare_and_fusion.3, pred[8]{0:T(512)(128)(4,1)S(1)} %get-tuple-element.331, ...), kind=kOutput, calls=%fused_computation.9.clone.1 | convolution fusion | flops 504496128 | bytes 8388628 | tf_op jit(solution)/shard_map/while/body/eval_jaxpr/sqji,spjk->spqik/dot_general | solution.py:47
  172.0 6.6 %copy.49 = f32[8,3,4,128,128]{4,3,2,1,0:T(8,128)} copy(f32[8,3,4,128,128]{3,4,2,1,0:T(8,128)} %convolution_bitcast_fusion.2) | data formatting | bytes 12582912 | tf_op jit(solution)/shard_map/while/body/eval_jaxpr/sqji,spjk->spqik/transpose | solution.py:47
  178.6 6.9 %reshape.248 = f32[24,65536]{1,0:T(8,128)} reshape(f32[8,3,4,128,128]{4,3,2,1,0:T(8,128)} %copy.49) | data formatting | bytes 12582912 | tf_op jit(solution)/shard_map/while/body/eval_jaxpr/reshape | solution.py:52
  185.5 4.0 %copy.50 = f32[3,8,512,128]{3,2,1,0:T(8,128)S(1)} copy(f32[3,8,512,128]{3,1,2,0:T(8,128)} %bitcast.89) | data formatting | bytes 12582912 | tf_op jit(solution)/shard_map/while
  189.5 7.4 %select_add_fusion.2 = f32[16,4,128,128]{3,0,2,1:T(8,128)S(1)} fusion(f32[16,4,128,128]{3,0,2,1:T(8,128)S(1)} %copy-done, f32[4,128,128,24]{2,1,0,3:T(8,128)S(1)} %bitcast.90, pred[]{:T(512)S(6)} %compare.7, s32[24]{0:T(128)S(1)} %select_n.208), kind=kOutput, calls=%fused_computation.8.clone.1 | convolution fusion | flops 304087424 | bytes 14680161 | tf_op jit(solution)/shard_map/while/body/eval_jaxpr/sj,sx->jx/dot_general | solution.py:54
  197.0 1.9 copy-done.1
  198.9 5.5 %copy.22 = f32[16,4,128,128]{3,2,1,0:T(8,128)} copy(f32[16,4,128,128]{3,0,2,1:T(8,128)} %get-tuple-element.204) | data formatting | bytes 8388608 | tf_op jit(solution)/shard_map/while | solution.py:86
  204.4 51.4 %reduce-scatter.2.cloned.1.call-done = f32[2,4,128,128]{3,2,1,0:T(8,128)} async-done(((f32[16,4,128,128]{3,2,1,0:T(8,128)}), f32[2,4,128,128]{3,2,1,0:T(8,128)}) %reduce-scatter.2.cloned.1.call-update) | async-done | bytes 524304 | tf_op jit(solution)/shard_map/reduce_scatter | solution.py:87
  (62 shorter events, 4.3 us)
Async XLA Ops:
  6.5 31.1 %all-gather.2.cloned.1.call-start = ((), (), s32[]{:S(2)}) async-start(), calls=%async_computation.1 | async-start | bytes 1769472 | tf_op jit(solution)/shard_map/all_gather | solution.py:24
  7.3 248.6 %reduce-scatter.2.cloned.1.call-start = ((), (), s32[]{:S(2)}) async-start(), calls=%async_computation.2 | async-start | bytes 4718592 | tf_op jit(solution)/shard_map/reduce_scatter | solution.py:87
  7.3 10.2 %collective-permute-start = (bf16[2,3,128,128]{3,2,1,0:T(8,128)(2,1)}, bf16[2,3,128,128]{3,2,1,0:T(8,128)(2,1)S(1)}, u32[]{:S(2)}, u32[]{:S(2)}) collective-permute-start(bf16[2,3,128,128]{3,2,1,0:T(8,128)(2,1)} %param.12), channel_id=1, source_target_pairs={{0,8},{8,16},{16,24},{24,0},{1,9},{9,17},{17,25},{25,1},{2,10},{10... | collective-permute-start | bytes 589832 | tf_op jit(solution)/shard_map/ppermute | solution.py:81
  17.5 7.9 %collective-permute-start.1 = (bf16[2,3,128,128]{3,2,1,0:T(8,128)(2,1)S(1)}, bf16[2,3,128,128]{3,2,1,0:T(8,128)(2,1)S(1)}, u32[]{:S(2)}, u32[]{:S(2)}) collective-permute-start(bf16[2,3,128,128]{3,2,1,0:T(8,128)(2,1)S(1)} %collective-permute-done), channel_id=1, source_target_pairs={{0,8},{8,16},{16,24},{24,0},{1,9},{9,17},{17,25},{25,1},{2,10},{10... | collective-permute-start | bytes 589832 | tf_op jit(solution)/shard_map/ppermute | solution.py:81
  25.4 7.5 %collective-permute-start.2 = (bf16[2,3,128,128]{3,2,1,0:T(8,128)(2,1)S(1)}, bf16[2,3,128,128]{3,2,1,0:T(8,128)(2,1)S(1)}, u32[]{:S(2)}, u32[]{:S(2)}) collective-permute-start(bf16[2,3,128,128]{3,2,1,0:T(8,128)(2,1)S(1)} %collective-permute-done.1), channel_id=1, source_target_pairs={{0,8},{8,16},{16,24},{24,0},{1,9},{9,17},{17,25},{25,1},{2,10},{10... | collective-permute-start | bytes 589832 | tf_op jit(solution)/shard_map/ppermute | solution.py:81
  64.6 4.0 %copy-start = (f32[16,4,128,128]{3,0,2,1:T(8,128)S(1)}, f32[16,4,128,128]{3,0,2,1:T(8,128)}, u32[]{:S(2)}) copy-start(f32[16,4,128,128]{3,0,2,1:T(8,128)} %get-tuple-element.346) | copy-start | bytes 12582916 | tf_op jit(solution)/shard_map/while
  76.0 1.9 copy-start.1
  104.9 4.0 %copy-start = (f32[16,4,128,128]{3,0,2,1:T(8,128)S(1)}, f32[16,4,128,128]{3,0,2,1:T(8,128)}, u32[]{:S(2)}) copy-start(f32[16,4,128,128]{3,0,2,1:T(8,128)} %get-tuple-element.346) | copy-start | bytes 12582916 | tf_op jit(solution)/shard_map/while
  116.3 1.9 copy-start.1
  145.2 4.0 %copy-start = (f32[16,4,128,128]{3,0,2,1:T(8,128)S(1)}, f32[16,4,128,128]{3,0,2,1:T(8,128)}, u32[]{:S(2)}) copy-start(f32[16,4,128,128]{3,0,2,1:T(8,128)} %get-tuple-element.346) | copy-start | bytes 12582916 | tf_op jit(solution)/shard_map/while
  156.6 1.9 copy-start.1
  185.5 4.0 %copy-start = (f32[16,4,128,128]{3,0,2,1:T(8,128)S(1)}, f32[16,4,128,128]{3,0,2,1:T(8,128)}, u32[]{:S(2)}) copy-start(f32[16,4,128,128]{3,0,2,1:T(8,128)} %get-tuple-element.346) | copy-start | bytes 12582916 | tf_op jit(solution)/shard_map/while
  196.9 1.9 copy-start.1
Sparse Core Ops, SparseCore 0:
  9.2 28.3 all-gather.1
  204.5 51.2 reduce-scatter.1
